TPU v7x, 32 devices: a whole 2x2x4 slice. The times are simulated.
32 devices in a mesh: kc: 8 (over z, core), ia: 4 (over y, x).
Axes of the slice: x: 2, y: 2, z: 4, core: 2. Of those that a mesh axis runs over, the one named last changes fastest.
Arguments:
- amplitudes: bfloat16 [32768, 32768], P('ia', 'kc'), may hold values from -0.03125 to 0.03125
- occupied_factors: bfloat16 [2048, 4096], P('kc'), may hold values from -0.1875 to 0.1875
- virtual_factors: bfloat16 [2048, 4096], P('kc', 'ia'), may hold values from -6 to 6
Outputs:
- residual: float32 [32768, 512], P('ia', 'kc')
All inputs are finite; a program needn't handle non-finite values.
Results may differ from a plain program's by a relative error of at most 0.0029.
Values may be sent and summed in bfloat16 or wider, within the bound.
A program may use at most 128 MiB of HBM per device.

v0:
```python
import jax
import jax.numpy as jnp
from jax import lax
from jax.sharding import PartitionSpec as P

O = 64
V = 512
BW = 8


def per_device(amplitudes, occupied_factors, virtual_factors):
    aux_local = occupied_factors.shape[0]
    k_per_device = O // lax.axis_size("kc")
    c_per_device = V // lax.axis_size("ia")
    shaped = occupied_factors.reshape(aux_local, O, O)
    regrouped = lax.all_to_all(shaped, "kc", split_axis=1, concat_axis=0, tiled=True)
    virtual_all = lax.all_gather(virtual_factors, "kc", axis=0, tiled=True)
    summed = lax.dot_general(
        regrouped.reshape(-1, k_per_device * O),
        virtual_all,
        (((0,), (0,)), ((), ())),
        preferred_element_type=jnp.float32,
    )
    integrals = summed.astype(jnp.bfloat16)
    blocks = (
        integrals.reshape(k_per_device, O, c_per_device, BW)
        .transpose(0, 2, 1, 3)
        .reshape(k_per_device, c_per_device, O * BW)
    )
    local_rows = amplitudes.shape[0]
    amplitude_view = amplitudes.reshape(local_rows, k_per_device, V)
    partial_sums = lax.dot_general(
        amplitude_view,
        lax.all_gather(blocks, "ia", axis=1, tiled=True),
        (((1, 2), (0, 1)), ((), ())),
        preferred_element_type=jnp.float32,
    )
    return lax.psum_scatter(partial_sums, "kc", scatter_dimension=1, tiled=True)


def solution(mesh):
    placed = (P("ia", "kc"), P("kc", None), P("kc", "ia"))
    return jax.shard_map(
        per_device, mesh=mesh, in_specs=placed, out_specs=P("ia", "kc"), check_vma=False
    )
```

profile of v0, /device:TPU:0, one launch (start us, length us, event | category | flops | bytes accessed | tf_op | source)
XLA Modules:
  0.0 381.7 jit_solution(13596248701743270473)
XLA Ops:
  6.5 0.0 all-gather.3.cloned.1.call-start
  6.5 0.7 all-gather.3.cloned.1.call-update
  7.3 0.0 all-gather.5.cloned.1.call-start
  7.3 3.3 copy.6
  10.6 88.9 %all_to_all.15 = bf16[256,64,64]{0,2,1:T(8,128)(2,1)S(1)} all-to-all(bf16[256,64,64]{0,2,1:T(8,128)(2,1)S(1)} %bitcast.28), channel_id=1, replica_groups=mesh['kc'=8,'ia'=4] {'kc'}, dimensions={1} | all-to-all | bytes 4194304 | tf_op jit(solution)/shard_map/all_to_all | solution.py:16
  99.5 1.3 copy.7
  100.8 0.7 copy.12
  101.5 0.0 all-gather.3.cloned.1.call-done
  101.5 5.5 %convolution_convert_fusion = bf16[512,1024]{1,0:T(8,128)(2,1)} fusion(bf16[2048,512]{0,1:T(8,128)(2,1)S(1)} %bitcast.30, bf16[2048,1024]{1,0:T(8,128)(2,1)} %all-gather.3.cloned.1.call-done), kind=kOutput, calls=%fused_computation.4 | convolution fusion | flops 2148007936 | bytes 7340032 | tf_op jit(solution)/shard_map/dot_general | solution.py:18
  107.0 1.5 copy.8
  108.5 1.1 reshape.18
  109.6 3.4 copy.9
  113.0 0.0 all-gather.5.cloned.1.call-update
  113.1 0.0 reduce-scatter.2.cloned.1.call-start
  113.1 51.5 %all-gather.5.cloned.1.call-done = bf16[8,512,512]{1,2,0:T(8,128)(2,1)} async-done(((bf16[8,128,512]{1,2,0:T(8,128)(2,1)}), bf16[8,512,512]{1,2,0:T(8,128)(2,1)}) %all-gather.5.cloned.1.call-update) | async-done | bytes 4194320 | tf_op jit(solution)/shard_map/all_gather | solution.py:34
  164.6 42.2 %fusion.3 = f32[8192,512]{0,1:T(8,128)} fusion(bf16[8,512,512]{1,2,0:T(8,128)(2,1)} %all-gather.5.cloned.1.call-done, bf16[1024,8,8,512]{3,2,1,0:T(8,128)(2,1)} %bitcast.8), kind=kOutput, calls=%fused_computation.3 | convolution fusion | flops 34359738368 | bytes 88080384 | tf_op jit(solution)/shard_map/dot_general | solution.py:32
  206.8 0.0 reduce-scatter.2.cloned.1.call-update
  206.8 168.3 %reduce-scatter.2.cloned.1.call-done = f32[8192,64]{0,1:T(8,128)} async-done(((f32[8192,512]{0,1:T(8,128)}), f32[8192,64]{0,1:T(8,128)}) %reduce-scatter.2.cloned.1.call-update) | async-done | bytes 2097168 | tf_op jit(solution)/shard_map/reduce_scatter | solution.py:38
Async XLA Ops:
  6.5 94.9 %all-gather.3.cloned.1.call-start = ((), (), s32[]{:S(2)}) async-start(), calls=%async_computation.2 | async-start | bytes 4718592 | tf_op jit(solution)/shard_map/all_gather | solution.py:17
  7.3 157.3 %all-gather.5.cloned.1.call-start = ((), (), s32[]{:S(2)}) async-start(), calls=%async_computation.3 | async-start | bytes 5242880 | tf_op jit(solution)/shard_map/all_gather | solution.py:34
  113.1 262.1 %reduce-scatter.2.cloned.1.call-start = ((), (), s32[]{:S(2)}) async-start(), calls=%async_computation.4 | async-start | bytes 18874368 | tf_op jit(solution)/shard_map/reduce_scatter | solution.py:38
Sparse Core Ops, SparseCore 0:
  8.9 88.0 all-gather.2
  113.2 51.3 all-gather.4
  206.9 168.1 reduce-scatter.1
where the time goes:
time: 382 us
  waiting for transfers between devices  221 us (58%)
  blocking collectives  88.9 us (23%)
  matrix products  47.7 us (12%)
  between operations  13.1 us (3%)
  local copies, waits for them, and re-layouts  11.3 us (3%)
    reduce_scatter x1, waiting for transfers between devices, per_device(): return lax.psum_scatter(partial_sums, 'kc', scatter_dimension=1, tiled=True)  168 us
    all_to_all x1, blocking collectives, per_device(): lax.all_to_all(shaped, 'kc', split_axis=1, concat_axis=0, tiled=True)  88.9 us
    all_gather x1, waiting for transfers between devices, per_device(): lax.all_gather(blocks, 'ia', axis=1, tiled=True)  51.5 us
    dot_general x1, matrix products, per_device(): lax.dot_general(amplitude_view, lax.all_gather(blocks, 'ia', axis=1, tile...  42.2 us
  transfers between devices with their start and end apart: 3, of which 2 were waited for; matrix products, arithmetic and copies ran while one was open for 1% of the time, Pallas kernels for 0%

commit v1 on v0

--- a/solution.py
+++ b/solution.py
@@ -1,11 +1,209 @@
+import functools
+
 import jax
 import jax.numpy as jnp
 from jax import lax
+from jax.experimental import pallas as pl
+from jax.experimental.pallas import tpu as pltpu
 from jax.sharding import PartitionSpec as P
 
 O = 64
 V = 512
 BW = 8
+MESH = pl.DeviceIdType.MESH
+
+
+def reduce_kernel(
+    n, count, rows, a_ref, b_ref, o_ref,
+    abuf, pair_out, pair_in, total, onward, from_left, from_right, kept, given,
+    a_sem, pair_s, pair_r, right_s, right_r, left_s, left_r, kept_sem, given_s, given_r,
+):
+    me = lax.axis_index("kc")
+    z, core = me // 2, me % 2
+    width = b_ref.shape[1] // n
+    half = width // 2
+    partner = z * 2 + (1 - core)
+    right, left = me + 2, me - 2
+
+    def fetch(t, own):
+        chunk = 2 * t + (core if own else 1 - core)
+        start = pl.multiple_of(chunk * rows, rows)
+        slot = 1 if own else 0
+        return pltpu.make_async_copy(a_ref.at[pl.ds(start, rows)], abuf.at[slot], a_sem.at[slot])
+
+    def pair(t):
+        return pltpu.make_async_remote_copy(
+            src_ref=pair_out.at[t], dst_ref=pair_in.at[t], send_sem=pair_s.at[t],
+            recv_sem=pair_r.at[t], device_id={"kc": partner}, device_id_type=MESH)
+
+    def go_right(t, d):
+        return pltpu.make_async_remote_copy(
+            src_ref=onward.at[t, d], dst_ref=from_left.at[t, d], send_sem=right_s.at[t, d],
+            recv_sem=right_r.at[t, d], device_id={"kc": right}, device_id_type=MESH)
+
+    def go_left(t, d):
+        return pltpu.make_async_remote_copy(
+            src_ref=onward.at[t, d], dst_ref=from_right.at[t, d], send_sem=left_s.at[t, d],
+            recv_sem=left_r.at[t, d], device_id={"kc": left}, device_id_type=MESH)
+
+    def keep(t):
+        start = pl.multiple_of((2 * t + core) * rows, rows)
+        return pltpu.make_async_copy(kept.at[t], o_ref.at[pl.ds(start, rows)], kept_sem.at[t])
+
+    def give(t, whose):
+        start = pl.multiple_of((2 * t + whose) * rows, rows)
+        return pltpu.make_async_remote_copy(
+            src_ref=given.at[t], dst_ref=o_ref.at[pl.ds(start, rows)], send_sem=given_s.at[t],
+            recv_sem=given_r.at[t], device_id={"kc": partner}, device_id_type=MESH)
+
+    fetch(0, False).start()
+    barrier = pltpu.get_barrier_semaphore()
+    pl.semaphore_signal(barrier, inc=1, device_id={"kc": partner}, device_id_type=MESH)
+
+    @pl.when(z > 0)
+    def _():
+        pl.semaphore_signal(barrier, inc=1, device_id={"kc": left}, device_id_type=MESH)
+
+    @pl.when(z < n - 1)
+    def _():
+        pl.semaphore_signal(barrier, inc=1, device_id={"kc": right}, device_id_type=MESH)
+
+    pl.semaphore_wait(barrier, 1 + jnp.where(z > 0, 1, 0) + jnp.where(z < n - 1, 1, 0))
+
+    def columns(t, d):
+        return total[t, :, d * width:(d + 1) * width]
+
+    def step(t, carry):
+        @pl.when(t < count)
+        def _():
+            fetch(t, False).wait()
+            fetch(t, True).start()
+            product = jnp.dot(abuf[0], b_ref[...], preferred_element_type=jnp.float32)
+            pair_out[t] = product.astype(jnp.bfloat16)
+            pair(t).start()
+            fetch(t, True).wait()
+
+            @pl.when(t + 1 < count)
+            def _():
+                fetch(t + 1, False).start()
+
+            total[t] = jnp.dot(abuf[1], b_ref[...], preferred_element_type=jnp.float32)
+            pair(t).wait_recv()
+            total[t] += pair_in[t].astype(jnp.float32)
+
+        tr = t - z
+
+        @pl.when((tr >= 0) & (tr < count))
+        def _():
+            for d in reversed(range(1, n)):
+                @pl.when((d > z) & (z == 0))
+                def _():
+                    onward[tr, d] = columns(tr, d).astype(jnp.bfloat16)
+                    go_right(tr, d).start()
+
+                @pl.when((d > z) & (z > 0))
+                def _():
+                    go_right(tr, d).wait_recv()
+                    onward[tr, d] = (columns(tr, d) + from_left[tr, d].astype(jnp.float32)).astype(jnp.bfloat16)
+                    go_right(tr, d).start()
+
+        tl = t - (n - 1 - z)
+
+        @pl.when((tl >= 0) & (tl < count))
+        def _():
+            for d in range(n - 1):
+                @pl.when((d < z) & (z == n - 1))
+                def _():
+                    onward[tl, d] = columns(tl, d).astype(jnp.bfloat16)
+                    go_left(tl, d).start()
+
+                @pl.when((d < z) & (z < n - 1))
+                def _():
+                    go_left(tl, d).wait_recv()
+                    onward[tl, d] = (columns(tl, d) + from_right[tl, d].astype(jnp.float32)).astype(jnp.bfloat16)
+                    go_left(tl, d).start()
+
+        tf = t - jnp.maximum(z, n - 1 - z)
+
+        @pl.when((tf >= 0) & (tf < count))
+        def _():
+            for d in range(n):
+                @pl.when(d == z)
+                def _():
+                    value = columns(tf, d)
+                    if d > 0:
+                        go_right(tf, d).wait_recv()
+                        value += from_left[tf, d].astype(jnp.float32)
+                    if d < n - 1:
+                        go_left(tf, d).wait_recv()
+                        value += from_right[tf, d].astype(jnp.float32)
+
+                    @pl.when(core == 0)
+                    def _():
+                        kept[tf] = value[:, :half]
+                        given[tf] = value[:, half:]
+
+                    @pl.when(core == 1)
+                    def _():
+                        kept[tf] = value[:, half:]
+                        given[tf] = value[:, :half]
+
+            keep(tf).start()
+            give(tf, core).start()
+
+        return carry
+
+    lax.fori_loop(0, count + n - 1, step, 0)
+
+    def drain(t, carry):
+        pair(t).wait_send()
+        keep(t).wait()
+        give(t, core).wait_send()
+        give(t, 1 - core).wait_recv()
+        for d in range(n):
+            @pl.when(d > z)
+            def _():
+                go_right(t, d).wait_send()
+
+            @pl.when(d < z)
+            def _():
+                go_left(t, d).wait_send()
+        return carry
+
+    lax.fori_loop(0, count, drain, 0)
+
+
+def gemm_reduce_scatter(amplitudes, cycle_block, devices):
+    local_rows, depth = amplitudes.shape
+    columns = cycle_block.shape[1]
+    n = devices // 2
+    rows = min(512, local_rows // 2)
+    count = local_rows // (2 * rows)
+    width = columns // n
+    bf, f32 = jnp.bfloat16, jnp.float32
+    dma = pltpu.SemaphoreType.DMA
+    return pl.pallas_call(
+        functools.partial(reduce_kernel, n, count, rows),
+        out_shape=jax.ShapeDtypeStruct((local_rows, width // 2), f32),
+        in_specs=[pl.BlockSpec(memory_space=pl.ANY), pl.BlockSpec(memory_space=pltpu.VMEM)],
+        out_specs=pl.BlockSpec(memory_space=pl.ANY),
+        scratch_shapes=[
+            pltpu.VMEM((2, rows, depth), bf),
+            pltpu.VMEM((count, rows, columns), bf),
+            pltpu.VMEM((count, rows, columns), bf),
+            pltpu.VMEM((count, rows, columns), f32),
+            pltpu.VMEM((count, n, rows, width), bf),
+            pltpu.VMEM((count, n, rows, width), bf),
+            pltpu.VMEM((count, n, rows, width), bf),
+            pltpu.VMEM((count, rows, width // 2), f32),
+            pltpu.VMEM((count, rows, width // 2), f32),
+            dma((2,)), dma((count,)), dma((count,)),
+            dma((count, n)), dma((count, n)), dma((count, n)), dma((count, n)),
+            dma((count,)), dma((count,)), dma((count,)),
+        ],
+        compiler_params=pltpu.CompilerParams(
+            collective_id=0, has_side_effects=True, vmem_limit_bytes=60 * 2**20),
+    )(amplitudes, cycle_block)
 
 
 def per_device(amplitudes, occupied_factors, virtual_factors):
@@ -27,15 +225,9 @@
         .transpose(0, 2, 1, 3)
         .reshape(k_per_device, c_per_device, O * BW)
     )
-    local_rows = amplitudes.shape[0]
-    amplitude_view = amplitudes.reshape(local_rows, k_per_device, V)
-    partial_sums = lax.dot_general(
-        amplitude_view,
-        lax.all_gather(blocks, "ia", axis=1, tiled=True),
-        (((1, 2), (0, 1)), ((), ())),
-        preferred_element_type=jnp.float32,
-    )
-    return lax.psum_scatter(partial_sums, "kc", scatter_dimension=1, tiled=True)
+    gathered = lax.all_gather(blocks, "ia", axis=1, tiled=True)
+    cycle_block = gathered.reshape(k_per_device * V, O * BW)
+    return gemm_reduce_scatter(amplitudes, cycle_block, lax.axis_size("kc"))
 
 
 def solution(mesh):

time: 382 us -> 269 us (0.70)
  waiting for transfers between devices: 221 us -> 52.3 us
  Pallas kernels: 0 us -> 87.1 us
  matrix products: 47.7 us -> 5.49 us
  local copies, waits for them, and re-layouts: 11.3 us -> 21.5 us
    reduce_scatter x1 -> x0, waiting for transfers between devices: 168 us -> none  [per_device(): return lax.psum_scatter(partial_sums, 'kc', scatter_dimension=1, tiled=True)]
    pallas_call x0 -> x1, Pallas kernels: none -> 87.1 us  [gemm_reduce_scatter(): pl.pallas_call(functools.partial(reduce_kernel, n, count, rows), out_shap...]
    dot_general x1 -> x0, matrix products: 42.2 us -> none  [per_device(): lax.dot_general(amplitude_view, lax.all_gather(blocks, 'ia', axis=1, tile...]
    all_gather x0 -> x1, local copies, waits for them, and re-layouts: none -> 6.46 us  [per_device(): gathered = lax.all_gather(blocks, 'ia', axis=1, tiled=True)]
  transfers between devices with their start and end apart: 3 -> 2, of which waited for: 2 -> 1; matrix products, arithmetic and copies ran while one was open for 1% -> 2% of each run, Pallas kernels for 0% -> 0%
where the time goes in v1:
time: 269 us
  blocking collectives  88.9 us (33%)
  Pallas kernels  87.1 us (32%)
  waiting for transfers between devices  52.3 us (19%)
  local copies, waits for them, and re-layouts  21.5 us (8%)
  between operations  13.5 us (5%)
  matrix products  5.49 us (2%)
    all_to_all x1, blocking collectives, per_device(): lax.all_to_all(shaped, 'kc', split_axis=1, concat_axis=0, tiled=True)  88.9 us
    pallas_call x1, Pallas kernels, gemm_reduce_scatter(): pl.pallas_call(functools.partial(reduce_kernel, n, count, rows), out_shap...  87.1 us
    all_gather x1, waiting for transfers between devices, per_device(): gathered = lax.all_gather(blocks, 'ia', axis=1, tiled=True)  51.5 us
    all_gather x1, local copies, waits for them, and re-layouts, per_device(): gathered = lax.all_gather(blocks, 'ia', axis=1, tiled=True)  6.46 us
    dot_general x1, matrix products, per_device(): lax.dot_general(regrouped.reshape(-1, k_per_device * O), virtual_all, (((...  5.49 us
  transfers between devices with their start and end apart: 2, of which 1 were waited for; matrix products, arithmetic and copies ran while one was open for 2% of the time, Pallas kernels for 0%

profile of v1, /device:TPU:0, one launch (start us, length us, event | category | flops | bytes accessed | tf_op | source)
XLA Modules:
  0.0 268.8 jit_solution(2028594465687340259)
XLA Ops:
  6.5 0.0 all-gather.3.cloned.1.call-start
  6.5 0.7 all-gather.3.cloned.1.call-update
  7.3 0.0 all-gather.5.cloned.1.call-start
  7.3 3.3 %copy.6 = bf16[256,4096]{0,1:T(8,128)(2,1)S(1)} copy(bf16[256,4096]{1,0:T(8,128)(2,1)} %param.4) | data formatting | bytes 4194304 | tf_op args[1]
  10.6 88.9 %all_to_all.15 = bf16[256,64,64]{0,2,1:T(8,128)(2,1)S(1)} all-to-all(bf16[256,64,64]{0,2,1:T(8,128)(2,1)S(1)} %bitcast.19), channel_id=1, replica_groups=mesh['kc'=8,'ia'=4] {'kc'}, dimensions={1} | all-to-all | bytes 4194304 | tf_op jit(solution)/shard_map/all_to_all | solution.py:214
  99.5 1.3 copy.7
  100.8 0.7 copy.12
  101.5 0.0 all-gather.3.cloned.1.call-done
  101.5 5.5 %convolution_convert_fusion = bf16[512,1024]{1,0:T(8,128)(2,1)} fusion(bf16[2048,512]{0,1:T(8,128)(2,1)S(1)} %bitcast.21, bf16[2048,1024]{1,0:T(8,128)(2,1)} %all-gather.3.cloned.1.call-done), kind=kOutput, calls=%fused_computation | convolution fusion | flops 2148007936 | bytes 7340032 | tf_op jit(solution)/shard_map/dot_general | solution.py:216
  107.0 1.5 copy.8
  108.5 1.1 reshape.18
  109.6 3.4 %copy.9 = bf16[8,128,64,8]{1,3,2,0:T(8,128)(2,1)} copy(bf16[8,128,64,8]{2,0,3,1:T(8,128)(2,1)S(1)} %bitcast.16) | data formatting | bytes 2097152 | tf_op jit(solution)/shard_map/transpose | solution.py:225
  113.0 0.0 all-gather.5.cloned.1.call-update
  113.1 51.5 %all-gather.5.cloned.1.call-done = bf16[8,512,512]{1,2,0:T(8,128)(2,1)} async-done(((bf16[8,128,512]{1,2,0:T(8,128)(2,1)}), bf16[8,512,512]{1,2,0:T(8,128)(2,1)}) %all-gather.5.cloned.1.call-update) | async-done | bytes 4194320 | tf_op jit(solution)/shard_map/all_gather | solution.py:228
  164.6 6.5 %copy.10 = bf16[8,512,512]{2,1,0:T(8,128)(2,1)} copy(bf16[8,512,512]{1,2,0:T(8,128)(2,1)} %all-gather.5.cloned.1.call-done) | data formatting | bytes 8388608 | tf_op jit(solution)/shard_map/all_gather | solution.py:228
  171.0 87.1 %shard_map.37 = f32[8192,64]{1,0:T(8,128)} custom-call(bf16[8192,4096]{1,0:T(8,128)(2,1)} %a_ref.1, bf16[4096,512]{1,0:T(8,128)(2,1)} %bitcast.15), custom_call_target="tpu_custom_call" | custom-call | tf_op jit(solution)/shard_map/pallas_call | solution.py:185
  258.2 3.8 %copy.11 = f32[8192,64]{0,1:T(8,128)} copy(f32[8192,64]{1,0:T(8,128)} %shard_map.37) | data formatting | bytes 4194304 | tf_op jit(solution)/shard_map/pallas_call | solution.py:185
Async XLA Ops:
  6.5 94.9 %all-gather.3.cloned.1.call-start = ((), (), s32[]{:S(2)}) async-start(), calls=%async_computation.1 | async-start | bytes 4718592 | tf_op jit(solution)/shard_map/all_gather | solution.py:215
  7.3 157.3 %all-gather.5.cloned.1.call-start = ((), (), s32[]{:S(2)}) async-start(), calls=%async_computation.2 | async-start | bytes 5242880 | tf_op jit(solution)/shard_map/all_gather | solution.py:228
Sparse Core Ops, SparseCore 0:
  8.9 88.0 all-gather.2
  113.2 51.3 all-gather.4

commit v2 on v1

--- a/solution.py
+++ b/solution.py
@@ -13,14 +13,228 @@
 MESH = pl.DeviceIdType.MESH
 
 
+class Spread:
+    def __init__(self, view, own, kind, groups, send, recv):
+        self.view, self.own, self.kind, self.send, self.recv = view, own, kind, send, recv
+        self.a = 2
+        self.b = groups // 2
+        me = lax.axis_index("ia")
+        self.p, self.q = me // self.b, me % self.b
+
+    def at(self, r, s):
+        return lax.rem(self.p + s + self.a, self.a) * self.b + lax.rem(self.q + r + self.b, self.b)
+
+    def copy(self, source, r, s, target):
+        return pltpu.make_async_remote_copy(
+            src_ref=self.view(self.at(*source)) if source != (0, 0) else self.own,
+            dst_ref=self.view(self.at(*source)), send_sem=self.send.at[r, s],
+            recv_sem=self.recv.at[r, s], device_id={"ia": self.at(*target)}, device_id_type=MESH)
+
+    def sends(self, direct):
+        out = []
+        for r in range(self.b):
+            for s in range(self.a):
+                if r and s and not direct:
+                    out.append(self.copy((-r, 0), r, s, (0, s)) if self.kind == 0
+                               else self.copy((0, -s), r, s, (r, 0)))
+                elif (r or s) and not (r and s) and direct:
+                    out.append(self.copy((0, 0), r, s, (r, s)))
+        return out
+
+    def arrived(self, r, s):
+        pltpu.make_async_remote_copy(
+            src_ref=self.view(self.at(-r, -s)), dst_ref=self.view(self.at(-r, -s)),
+            send_sem=self.send.at[r, s], recv_sem=self.recv.at[r, s],
+            device_id={"ia": self.at(r, s)}, device_id_type=MESH).wait_recv()
+
+    def start(self):
+        order = self.sends(True)
+        for copy in order if self.kind else reversed(order):
+            copy.start()
+
+    def relay(self):
+        if self.kind == 0:
+            for r in range(1, self.b):
+                self.arrived(r, 0)
+        else:
+            for s in range(1, self.a):
+                self.arrived(0, s)
+        for copy in self.sends(False):
+            copy.start()
+
+    def finish(self):
+        for r in range(self.b):
+            for s in range(self.a):
+                first = (s == 0) if self.kind == 0 else (r == 0)
+                if (r or s) and not first:
+                    self.arrived(r, s)
+
+    def drain(self):
+        for copy in self.sends(True) + self.sends(False):
+            copy.wait_send()
+
+
+def signal_all(barrier, axis, size):
+    me = lax.axis_index(axis)
+    for step in range(1, size):
+        pl.semaphore_signal(barrier, inc=1, device_id={axis: lax.rem(me + step, size)}, device_id_type=MESH)
+
+
+def factors_kernel(
+    devices, groups, occ_ref, virt_ref, out_ref, occ, virt,
+    o_s, o_r, g_s, g_r, right_s, left_s, v_r, pair_s, pair_r,
+):
+    n = devices // 2
+    me, ia = lax.axis_index("kc"), lax.axis_index("ia")
+    z, core = me // 2, me % 2
+    share = occ_ref.shape[0] // groups
+    cols = occ_ref.shape[1] // devices
+
+    barrier = pltpu.get_barrier_semaphore()
+    signal_all(barrier, "kc", devices)
+    signal_all(barrier, "ia", groups)
+    pl.semaphore_wait(barrier, devices + groups - 2)
+
+    def direct(step):
+        to = lax.rem(me + step, devices)
+        return pltpu.make_async_remote_copy(
+            src_ref=occ_ref.at[pl.ds(pl.multiple_of(ia * share, share), share),
+                               pl.ds(pl.multiple_of(to * cols, cols), cols)],
+            dst_ref=occ.at[me, ia], send_sem=o_s.at[step], recv_sem=o_r.at[step],
+            device_id={"kc": to}, device_id_type=MESH)
+
+    def came(step):
+        source = lax.rem(me - step + devices, devices)
+        pltpu.make_async_remote_copy(
+            src_ref=occ.at[source, ia], dst_ref=occ.at[source, ia], send_sem=o_s.at[step],
+            recv_sem=o_r.at[step], device_id={"kc": source}, device_id_type=MESH).wait_recv()
+
+    def virtual(chip, way, own=False):
+        place = virt.at[chip * 2 + core]
+        send = {"right": right_s, "left": left_s, "pair": pair_s}[way]
+        to = {"right": me + 2, "left": me - 2, "pair": z * 2 + 1 - core}[way]
+        recv = pair_r if way == "pair" else v_r
+        return pltpu.make_async_remote_copy(
+            src_ref=virt_ref if own else place, dst_ref=place, send_sem=send.at[chip],
+            recv_sem=recv.at[chip], device_id={"kc": to}, device_id_type=MESH)
+
+    @pl.when(z < n - 1)
+    def _():
+        virtual(z, "right", True).start()
+
+    @pl.when(z > 0)
+    def _():
+        virtual(z, "left", True).start()
+
+    for step in range(1, devices):
+        direct(step).start()
+    virtual(z, "pair", True).start()
+    virt[me] = virt_ref[...]
+    for q in range(groups):
+        occ[me, q] = occ_ref[q * share:(q + 1) * share, pl.ds(pl.multiple_of(me * cols, cols), cols)]
+
+    spreads = []
+    for step in range(1, devices):
+        source = lax.rem(me - step + devices, devices)
+        view = functools.partial(lambda source, i: occ.at[source, i], source)
+        spreads.append(Spread(view, view(ia), step % 2, groups, g_s.at[step], g_r.at[step]))
+
+    def hop(step):
+        @pl.when(z - step >= 0)
+        def _():
+            virtual(z - step, "left").wait_recv()
+
+            @pl.when(z < n - 1)
+            def _():
+                virtual(z - step, "right").start()
+
+            virtual(z - step, "pair").start()
+
+        @pl.when(z + step < n)
+        def _():
+            virtual(z + step, "left").wait_recv()
+
+            @pl.when(z > 0)
+            def _():
+                virtual(z + step, "left").start()
+
+            virtual(z + step, "pair").start()
+
+    for step in range(1, devices):
+        came(step)
+        spreads[step - 1].start()
+    hop(1)
+    for spread in spreads:
+        spread.relay()
+    for step in range(2, n):
+        hop(step)
+    for spread in spreads:
+        spread.finish()
+    for chip in range(n):
+        place = virt.at[chip * 2 + 1 - core]
+        pltpu.make_async_remote_copy(
+            src_ref=place, dst_ref=place, send_sem=pair_s.at[chip], recv_sem=pair_r.at[chip],
+            device_id={"kc": z * 2 + 1 - core}, device_id_type=MESH).wait_recv()
+
+    block = min(256, out_ref.shape[0])
+    depth = devices * occ_ref.shape[0]
+
+    def multiply(i, carry):
+        at = pl.ds(pl.multiple_of(i * block, block), block)
+        product = lax.dot_general(
+            virt[:, :, at].reshape(depth, block), occ[...].reshape(depth, cols),
+            (((0,), (0,)), ((), ())), preferred_element_type=jnp.float32)
+        out_ref[at, :] = product.astype(jnp.bfloat16)
+        return carry
+
+    lax.fori_loop(0, out_ref.shape[0] // block, multiply, 0)
+
+    for step in range(1, devices):
+        direct(step).wait_send()
+        spreads[step - 1].drain()
+    for chip in range(n):
+        virtual(chip, "pair").wait_send()
+
+        @pl.when((chip <= z) & (z < n - 1))
+        def _():
+            virtual(chip, "right").wait_send()
+
+        @pl.when((chip >= z) & (z > 0))
+        def _():
+            virtual(chip, "left").wait_send()
+
+
+def transposed_integrals(occupied, virtual, devices, groups):
+    share, cols = occupied.shape[0] // groups, occupied.shape[1] // devices
+    n = devices // 2
+    bf = jnp.bfloat16
+    dma = pltpu.SemaphoreType.DMA
+    vmem = pl.BlockSpec(memory_space=pltpu.VMEM)
+    return pl.pallas_call(
+        functools.partial(factors_kernel, devices, groups),
+        out_shape=jax.ShapeDtypeStruct((virtual.shape[1], cols), bf),
+        in_specs=[vmem, vmem],
+        out_specs=vmem,
+        scratch_shapes=[
+            pltpu.VMEM((devices, groups, share, cols), bf),
+            pltpu.VMEM((devices,) + virtual.shape, bf),
+            dma((devices,)), dma((devices,)),
+            dma((devices, groups // 2, 2)), dma((devices, groups // 2, 2)),
+            dma((n,)), dma((n,)), dma((n,)), dma((n,)), dma((n,)),
+        ],
+        compiler_params=pltpu.CompilerParams(
+            collective_id=1, has_side_effects=True, vmem_limit_bytes=40 * 2**20),
+    )(occupied, virtual)
+
+
 def reduce_kernel(
-    n, count, rows, a_ref, b_ref, o_ref,
-    abuf, pair_out, pair_in, total, onward, from_left, from_right, kept, given,
-    a_sem, pair_s, pair_r, right_s, right_r, left_s, left_r, kept_sem, given_s, given_r,
+    n, groups, count, rows, a_ref, own_ref, o_ref,
+    gathered, abuf, pair_out, pair_in, total, onward, from_left, from_right, kept, given,
+    a_sem, pair_s, pair_r, right_s, right_r, left_s, left_r, kept_sem, given_s, given_r, g_s, g_r,
 ):
     me = lax.axis_index("kc")
     z, core = me // 2, me % 2
-    width = b_ref.shape[1] // n
+    width = own_ref.shape[2] // n
     half = width // 2
     partner = z * 2 + (1 - core)
     right, left = me + 2, me - 2
@@ -56,6 +270,14 @@
             src_ref=given.at[t], dst_ref=o_ref.at[pl.ds(start, rows)], send_sem=given_s.at[t],
             recv_sem=given_r.at[t], device_id={"kc": partner}, device_id_type=MESH)
 
+    ia = lax.axis_index("ia")
+    k_half = own_ref.shape[0] // 2
+    spreads = []
+    for kind in range(2):
+        ks = pl.ds(kind * k_half, k_half)
+        view = functools.partial(lambda ks, i: gathered.at[ks, i], ks)
+        spreads.append(Spread(view, own_ref.at[ks], kind, groups, g_s.at[kind], g_r.at[kind]))
+
     fetch(0, False).start()
     barrier = pltpu.get_barrier_semaphore()
     pl.semaphore_signal(barrier, inc=1, device_id={"kc": partner}, device_id_type=MESH)
@@ -68,7 +290,19 @@
     def _():
         pl.semaphore_signal(barrier, inc=1, device_id={"kc": right}, device_id_type=MESH)
 
-    pl.semaphore_wait(barrier, 1 + jnp.where(z > 0, 1, 0) + jnp.where(z < n - 1, 1, 0))
+    signal_all(barrier, "ia", groups)
+    pl.semaphore_wait(barrier, groups + jnp.where(z > 0, 1, 0) + jnp.where(z < n - 1, 1, 0))
+    for spread in spreads:
+        spread.start()
+    for k in range(own_ref.shape[0]):
+        gathered[k, ia] = own_ref[k]
+    for spread in spreads:
+        spread.relay()
+    for spread in spreads:
+        spread.finish()
+
+    def cycle():
+        return gathered[...].reshape(-1, own_ref.shape[2])
 
     def columns(t, d):
         return total[t, :, d * width:(d + 1) * width]
@@ -78,7 +312,7 @@
         def _():
             fetch(t, False).wait()
             fetch(t, True).start()
-            product = jnp.dot(abuf[0], b_ref[...], preferred_element_type=jnp.float32)
+            product = jnp.dot(abuf[0], cycle(), preferred_element_type=jnp.float32)
             pair_out[t] = product.astype(jnp.bfloat16)
             pair(t).start()
             fetch(t, True).wait()
@@ -87,7 +321,7 @@
             def _():
                 fetch(t + 1, False).start()
 
-            total[t] = jnp.dot(abuf[1], b_ref[...], preferred_element_type=jnp.float32)
+            total[t] = jnp.dot(abuf[1], cycle(), preferred_element_type=jnp.float32)
             pair(t).wait_recv()
             total[t] += pair_in[t].astype(jnp.float32)
 
@@ -171,11 +405,13 @@
         return carry
 
     lax.fori_loop(0, count, drain, 0)
-
-
-def gemm_reduce_scatter(amplitudes, cycle_block, devices):
+    for spread in spreads:
+        spread.drain()
+
+
+def gemm_reduce_scatter(amplitudes, blocks, devices, groups):
     local_rows, depth = amplitudes.shape
-    columns = cycle_block.shape[1]
+    columns = blocks.shape[2]
     n = devices // 2
     rows = min(512, local_rows // 2)
     count = local_rows // (2 * rows)
@@ -183,11 +419,12 @@
     bf, f32 = jnp.bfloat16, jnp.float32
     dma = pltpu.SemaphoreType.DMA
     return pl.pallas_call(
-        functools.partial(reduce_kernel, n, count, rows),
+        functools.partial(reduce_kernel, n, groups, count, rows),
         out_shape=jax.ShapeDtypeStruct((local_rows, width // 2), f32),
         in_specs=[pl.BlockSpec(memory_space=pl.ANY), pl.BlockSpec(memory_space=pltpu.VMEM)],
         out_specs=pl.BlockSpec(memory_space=pl.ANY),
         scratch_shapes=[
+            pltpu.VMEM((blocks.shape[0], groups, blocks.shape[1], columns), bf),
             pltpu.VMEM((2, rows, depth), bf),
             pltpu.VMEM((count, rows, columns), bf),
             pltpu.VMEM((count, rows, columns), bf),
@@ -200,34 +437,24 @@
             dma((2,)), dma((count,)), dma((count,)),
             dma((count, n)), dma((count, n)), dma((count, n)), dma((count, n)),
             dma((count,)), dma((count,)), dma((count,)),
+            dma((2, groups // 2, 2)), dma((2, groups // 2, 2)),
         ],
         compiler_params=pltpu.CompilerParams(
             collective_id=0, has_side_effects=True, vmem_limit_bytes=60 * 2**20),
-    )(amplitudes, cycle_block)
+    )(amplitudes, blocks)
 
 
 def per_device(amplitudes, occupied_factors, virtual_factors):
-    aux_local = occupied_factors.shape[0]
-    k_per_device = O // lax.axis_size("kc")
-    c_per_device = V // lax.axis_size("ia")
-    shaped = occupied_factors.reshape(aux_local, O, O)
-    regrouped = lax.all_to_all(shaped, "kc", split_axis=1, concat_axis=0, tiled=True)
-    virtual_all = lax.all_gather(virtual_factors, "kc", axis=0, tiled=True)
-    summed = lax.dot_general(
-        regrouped.reshape(-1, k_per_device * O),
-        virtual_all,
-        (((0,), (0,)), ((), ())),
-        preferred_element_type=jnp.float32,
-    )
-    integrals = summed.astype(jnp.bfloat16)
+    devices, groups = lax.axis_size("kc"), lax.axis_size("ia")
+    k_per_device = O // devices
+    c_per_device = V // groups
+    integrals = transposed_integrals(occupied_factors, virtual_factors, devices, groups)
     blocks = (
-        integrals.reshape(k_per_device, O, c_per_device, BW)
-        .transpose(0, 2, 1, 3)
+        integrals.reshape(c_per_device, BW, k_per_device, O)
+        .transpose(2, 0, 3, 1)
         .reshape(k_per_device, c_per_device, O * BW)
     )
-    gathered = lax.all_gather(blocks, "ia", axis=1, tiled=True)
-    cycle_block = gathered.reshape(k_per_device * V, O * BW)
-    return gemm_reduce_scatter(amplitudes, cycle_block, lax.axis_size("kc"))
+    return gemm_reduce_scatter(amplitudes, blocks, devices, groups)
 
 
 def solution(mesh):

time: 269 us -> 194 us (0.72)
  Pallas kernels: 87.1 us -> 183 us
  blocking collectives: 88.9 us -> 0 us
  waiting for transfers between devices: 52.3 us -> 0 us
  between operations: 13.5 us -> 0.03 us
  local copies, waits for them, and re-layouts: 21.5 us -> 11.3 us
  matrix products: 5.49 us -> 0 us
    pallas_call x1 -> x2, Pallas kernels: 87.1 us -> 183 us  [the longest x1 125 us: gemm_reduce_scatter(): pl.pallas_call(functools.partial(reduce_kernel, n, groups, count, rows),...]
    all_to_all x1 -> x0, blocking collectives: 88.9 us -> none  [per_device(): lax.all_to_all(shaped, 'kc', split_axis=1, concat_axis=0, tiled=True)]
    all_gather x2 -> x0, waiting for transfers between devices: 51.6 us -> none  [the longest x1 51.5 us: per_device(): gathered = lax.all_gather(blocks, 'ia', axis=1, tiled=True)]
    all_gather x1 -> x0, local copies, waits for them, and re-layouts: 6.46 us -> none  [per_device(): gathered = lax.all_gather(blocks, 'ia', axis=1, tiled=True)]
    dot_general x1 -> x0, matrix products: 5.49 us -> none  [per_device(): lax.dot_general(regrouped.reshape(-1, k_per_device * O), virtual_all, (((...]
  transfers between devices with their start and end apart: 2 -> 0, of which waited for: 1 -> 0; matrix products, arithmetic and copies ran while one was open for 2% -> 0% of each run, Pallas kernels for 0% -> 0%
where the time goes in v2:
time: 194 us
  Pallas kernels  183 us (94%)
  local copies, waits for them, and re-layouts  11.3 us (6%)
    pallas_call x1, Pallas kernels, gemm_reduce_scatter(): pl.pallas_call(functools.partial(reduce_kernel, n, groups, count, rows),...  125 us
    pallas_call x1, Pallas kernels, transposed_integrals(): pl.pallas_call(functools.partial(factors_kernel, devices, groups), out_sh...  58.1 us

profile of v2, /device:TPU:0, one launch (start us, length us, event | category | flops | bytes accessed | tf_op | source)
XLA Modules:
  0.0 194.1 jit_solution(4442819874361338542)
XLA Ops:
  0.0 0.0 copy-start
  0.0 1.6 copy-done
  1.6 0.0 copy-start.1
  1.6 1.0 copy-done.1
  2.6 58.1 %shard_map.37 = bf16[1024,512]{1,0:T(8,128)(2,1)S(1)} custom-call(bf16[256,4096]{1,0:T(8,128)(2,1)S(1)} %copy-done, bf16[256,1024]{1,0:T(8,128)(2,1)S(1)} %copy-done.1), custom_call_target="tpu_custom_call" | custom-call | tf_op jit(solution)/shard_map/pallas_call | solution.py:213
  60.7 1.1 reshape.6
  61.8 2.5 %copy.6 = bf16[8,128,64,8]{1,3,2,0:T(8,128)(2,1)S(1)} copy(bf16[8,128,64,8]{2,0,3,1:T(8,128)(2,1)S(1)} %bitcast.2) | data formatting | bytes 2097152 | tf_op jit(solution)/shard_map/transpose | solution.py:454
  64.3 1.3 copy.7.own_ref
  65.7 124.6 %shard_map.38 = f32[8192,64]{1,0:T(8,128)} custom-call(bf16[8192,4096]{1,0:T(8,128)(2,1)} %a_ref.1, bf16[8,128,512]{2,1,0:T(8,128)(2,1)} %copy.7.own_ref), custom_call_target="tpu_custom_call" | custom-call | tf_op jit(solution)/shard_map/pallas_call | solution.py:421
  190.3 3.8 %copy.8 = f32[8192,64]{0,1:T(8,128)} copy(f32[8192,64]{1,0:T(8,128)} %shard_map.38) | data formatting | bytes 4194304 | tf_op jit(solution)/shard_map/pallas_call | solution.py:421
Async XLA Ops:
  0.0 1.6 copy-start
  1.6 1.0 copy-start.1

commit v3 on v2

--- a/solution.py
+++ b/solution.py
@@ -262,12 +262,12 @@
 
     def keep(t):
         start = pl.multiple_of((2 * t + core) * rows, rows)
-        return pltpu.make_async_copy(kept.at[t], o_ref.at[pl.ds(start, rows)], kept_sem.at[t])
+        return pltpu.make_async_copy(kept.at[t], o_ref.at[:, pl.ds(start, rows)], kept_sem.at[t])
 
     def give(t, whose):
         start = pl.multiple_of((2 * t + whose) * rows, rows)
         return pltpu.make_async_remote_copy(
-            src_ref=given.at[t], dst_ref=o_ref.at[pl.ds(start, rows)], send_sem=given_s.at[t],
+            src_ref=given.at[t], dst_ref=o_ref.at[:, pl.ds(start, rows)], send_sem=given_s.at[t],
             recv_sem=given_r.at[t], device_id={"kc": partner}, device_id_type=MESH)
 
     ia = lax.axis_index("ia")
@@ -372,15 +372,17 @@
                         go_left(tf, d).wait_recv()
                         value += from_right[tf, d].astype(jnp.float32)
 
+                    value = value.T
+
                     @pl.when(core == 0)
                     def _():
-                        kept[tf] = value[:, :half]
-                        given[tf] = value[:, half:]
+                        kept[tf] = value[:half]
+                        given[tf] = value[half:]
 
                     @pl.when(core == 1)
                     def _():
-                        kept[tf] = value[:, half:]
-                        given[tf] = value[:, :half]
+                        kept[tf] = value[half:]
+                        given[tf] = value[:half]
 
             keep(tf).start()
             give(tf, core).start()
@@ -413,14 +415,14 @@
     local_rows, depth = amplitudes.shape
     columns = blocks.shape[2]
     n = devices // 2
-    rows = min(512, local_rows // 2)
+    rows = min(256, local_rows // 2)
     count = local_rows // (2 * rows)
     width = columns // n
     bf, f32 = jnp.bfloat16, jnp.float32
     dma = pltpu.SemaphoreType.DMA
     return pl.pallas_call(
         functools.partial(reduce_kernel, n, groups, count, rows),
-        out_shape=jax.ShapeDtypeStruct((local_rows, width // 2), f32),
+        out_shape=jax.ShapeDtypeStruct((width // 2, local_rows), f32),
         in_specs=[pl.BlockSpec(memory_space=pl.ANY), pl.BlockSpec(memory_space=pltpu.VMEM)],
         out_specs=pl.BlockSpec(memory_space=pl.ANY),
         scratch_shapes=[
@@ -432,8 +434,8 @@
             pltpu.VMEM((count, n, rows, width), bf),
             pltpu.VMEM((count, n, rows, width), bf),
             pltpu.VMEM((count, n, rows, width), bf),
-            pltpu.VMEM((count, rows, width // 2), f32),
-            pltpu.VMEM((count, rows, width // 2), f32),
+            pltpu.VMEM((count, width // 2, rows), f32),
+            pltpu.VMEM((count, width // 2, rows), f32),
             dma((2,)), dma((count,)), dma((count,)),
             dma((count, n)), dma((count, n)), dma((count, n)), dma((count, n)),
             dma((count,)), dma((count,)), dma((count,)),
@@ -441,7 +443,7 @@
         ],
         compiler_params=pltpu.CompilerParams(
             collective_id=0, has_side_effects=True, vmem_limit_bytes=60 * 2**20),
-    )(amplitudes, blocks)
+    )(amplitudes, blocks).T
 
 
 def per_device(amplitudes, occupied_factors, virtual_factors):

time: 194 us -> 194 us (level)
    pallas_call x1 -> x0, local copies, waits for them, and re-layouts: 3.79 us -> none  [gemm_reduce_scatter(): pl.pallas_call(functools.partial(reduce_kernel, n, groups, count, rows),...]
    unnamed x4 -> x5, local copies, waits for them, and re-layouts: 2.63 us -> 5.69 us
where the time goes in v3:
time: 194 us; the launch traced here: 193 us
  Pallas kernels  182 us (94%)
  local copies, waits for them, and re-layouts  10.6 us (5%)
    pallas_call x1, Pallas kernels, gemm_reduce_scatter(): pl.pallas_call(functools.partial(reduce_kernel, n, groups, count, rows),...  124 us
    pallas_call x1, Pallas kernels, transposed_integrals(): pl.pallas_call(functools.partial(factors_kernel, devices, groups), out_sh...  58.1 us
    unnamed x5, local copies, waits for them, and re-layouts  5.69 us

profile of v3, /device:TPU:0, one launch (start us, length us, event | category | flops | bytes accessed | tf_op | source)
XLA Modules:
  0.0 192.7 jit_solution(4253372635419514481)
XLA Ops:
  0.0 0.0 copy-start
  0.0 1.6 copy-done
  1.6 0.0 copy-start.1
  1.6 1.0 copy-done.1
  2.6 58.1 %shard_map.37 = bf16[1024,512]{1,0:T(8,128)(2,1)S(1)} custom-call(bf16[256,4096]{1,0:T(8,128)(2,1)S(1)} %copy-done, bf16[256,1024]{1,0:T(8,128)(2,1)S(1)} %copy-done.1), custom_call_target="tpu_custom_call" | custom-call | tf_op jit(solution)/shard_map/pallas_call | solution.py:213
  60.7 1.1 reshape.6
  61.8 2.5 %copy.5 = bf16[8,128,64,8]{1,3,2,0:T(8,128)(2,1)S(1)} copy(bf16[8,128,64,8]{2,0,3,1:T(8,128)(2,1)S(1)} %bitcast.4) | data formatting | bytes 2097152 | tf_op jit(solution)/shard_map/transpose | solution.py:456
  64.3 1.3 copy.6.own_ref
  65.7 124.0 %shard_map.38 = f32[64,8192]{1,0:T(8,128)} custom-call(bf16[8192,4096]{1,0:T(8,128)(2,1)} %a_ref.1, bf16[8,128,512]{2,1,0:T(8,128)(2,1)} %copy.6.own_ref), custom_call_target="tpu_custom_call" | custom-call | tf_op jit(solution)/shard_map/pallas_call | solution.py:423
  189.6 3.1 %copy.8 = f32[8192,64]{0,1:T(8,128)} copy(f32[8192,64]{0,1:T(8,128)} %bitcast.3) | data formatting | bytes 4194304
Async XLA Ops:
  0.0 1.6 copy-start
  1.6 1.0 copy-start.1

commit v4 on v3

--- a/solution.py
+++ b/solution.py
@@ -81,8 +81,8 @@
 
 
 def factors_kernel(
-    devices, groups, occ_ref, virt_ref, out_ref, occ, virt,
-    o_s, o_r, g_s, g_r, right_s, left_s, v_r, pair_s, pair_r,
+    devices, groups, occ_ref, virt_ref, out_ref, occ, virt, total,
+    o_s, o_r, g_s, g_r, right_s, left_s, v_r, pair_s, pair_r, mine_s,
 ):
     n = devices // 2
     me, ia = lax.axis_index("kc"), lax.axis_index("ia")
@@ -129,9 +129,14 @@
     for step in range(1, devices):
         direct(step).start()
     virtual(z, "pair", True).start()
-    virt[me] = virt_ref[...]
+    mine = [pltpu.make_async_copy(virt_ref, virt.at[me], mine_s.at[groups])]
     for q in range(groups):
-        occ[me, q] = occ_ref[q * share:(q + 1) * share, pl.ds(pl.multiple_of(me * cols, cols), cols)]
+        mine.append(pltpu.make_async_copy(
+            occ_ref.at[pl.ds(q * share, share), pl.ds(pl.multiple_of(me * cols, cols), cols)],
+            occ.at[me, q], mine_s.at[q]))
+    for copy in mine:
+        copy.start()
+    total[...] = jnp.zeros_like(total)
 
     spreads = []
     for step in range(1, devices):
@@ -166,28 +171,44 @@
     hop(1)
     for spread in spreads:
         spread.relay()
-    for step in range(2, n):
+    for step in range(2, n - 1):
         hop(step)
     for spread in spreads:
         spread.finish()
-    for chip in range(n):
+    for copy in mine:
+        copy.wait()
+    block = min(256, out_ref.shape[0])
+    depth = 2 * occ_ref.shape[0]
+
+    def add_chip(chip):
         place = virt.at[chip * 2 + 1 - core]
         pltpu.make_async_remote_copy(
             src_ref=place, dst_ref=place, send_sem=pair_s.at[chip], recv_sem=pair_r.at[chip],
             device_id={"kc": z * 2 + 1 - core}, device_id_type=MESH).wait_recv()
-
-    block = min(256, out_ref.shape[0])
-    depth = devices * occ_ref.shape[0]
-
-    def multiply(i, carry):
-        at = pl.ds(pl.multiple_of(i * block, block), block)
-        product = lax.dot_general(
-            virt[:, :, at].reshape(depth, block), occ[...].reshape(depth, cols),
-            (((0,), (0,)), ((), ())), preferred_element_type=jnp.float32)
-        out_ref[at, :] = product.astype(jnp.bfloat16)
-        return carry
-
-    lax.fori_loop(0, out_ref.shape[0] // block, multiply, 0)
+        rows = slice(2 * chip, 2 * chip + 2)
+
+        def multiply(i, carry):
+            at = pl.ds(pl.multiple_of(i * block, block), block)
+            total[at, :] += lax.dot_general(
+                virt[rows, :, at].reshape(depth, block), occ[rows].reshape(depth, cols),
+                (((0,), (0,)), ((), ())), preferred_element_type=jnp.float32)
+            return carry
+
+        lax.fori_loop(0, out_ref.shape[0] // block, multiply, 0)
+
+    for chip in range(n):
+        @pl.when((chip - z < n - 1) & (z - chip < n - 1))
+        def _():
+            add_chip(chip)
+
+    if n > 2:
+        hop(n - 1)
+    for chip in (0, n - 1):
+        @pl.when((chip - z == n - 1) | (z - chip == n - 1))
+        def _():
+            add_chip(chip)
+
+    out_ref[...] = total[...].astype(jnp.bfloat16)
 
     for step in range(1, devices):
         direct(step).wait_send()
@@ -213,17 +234,18 @@
     return pl.pallas_call(
         functools.partial(factors_kernel, devices, groups),
         out_shape=jax.ShapeDtypeStruct((virtual.shape[1], cols), bf),
-        in_specs=[vmem, vmem],
+        in_specs=[pl.BlockSpec(memory_space=pl.ANY)] * 2,
         out_specs=vmem,
         scratch_shapes=[
             pltpu.VMEM((devices, groups, share, cols), bf),
             pltpu.VMEM((devices,) + virtual.shape, bf),
+            pltpu.VMEM((virtual.shape[1], cols), jnp.float32),
             dma((devices,)), dma((devices,)),
             dma((devices, groups // 2, 2)), dma((devices, groups // 2, 2)),
-            dma((n,)), dma((n,)), dma((n,)), dma((n,)), dma((n,)),
+            dma((n,)), dma((n,)), dma((n,)), dma((n,)), dma((n,)), dma((groups + 1,)),
         ],
         compiler_params=pltpu.CompilerParams(
-            collective_id=1, has_side_effects=True, vmem_limit_bytes=40 * 2**20),
+            collective_id=1, has_side_effects=True, vmem_limit_bytes=60 * 2**20),
     )(occupied, virtual)
 
 

time: 194 us -> 192 us (0.990)
    unnamed x5 -> x1, local copies, waits for them, and re-layouts: 5.69 us -> 3.06 us
where the time goes in v4:
time: 192 us; the launch traced here: 191 us
  Pallas kernels  182 us (95%)
  local copies, waits for them, and re-layouts  9.67 us (5%)
    pallas_call x1, Pallas kernels, gemm_reduce_scatter(): pl.pallas_call(functools.partial(reduce_kernel, n, groups, count, rows),...  124 us
    pallas_call x1, Pallas kernels, transposed_integrals(): pl.pallas_call(functools.partial(factors_kernel, devices, groups), out_sh...  57.8 us

profile of v4, /device:TPU:0, one launch (start us, length us, event | category | flops | bytes accessed | tf_op | source)
XLA Modules:
  0.0 191.4 jit_solution(14783342138861814386)
XLA Ops:
  0.0 57.8 %shard_map.37 = bf16[1024,512]{1,0:T(8,128)(2,1)} custom-call(bf16[256,4096]{1,0:T(8,128)(2,1)} %occ_ref.1, bf16[256,1024]{1,0:T(8,128)(2,1)} %virt_ref.1), custom_call_target="tpu_custom_call" | custom-call | tf_op jit(solution)/shard_map/pallas_call | solution.py:234
  57.8 2.8 %reshape.6 = bf16[128,8,8,64]{3,2,1,0:T(8,128)(2,1)S(1)} reshape(bf16[1024,512]{1,0:T(8,128)(2,1)} %shard_map.37) | data formatting | bytes 2097152 | tf_op jit(solution)/shard_map/reshape | solution.py:477
  60.6 2.5 %copy.5 = bf16[8,128,64,8]{1,3,2,0:T(8,128)(2,1)S(1)} copy(bf16[8,128,64,8]{2,0,3,1:T(8,128)(2,1)S(1)} %bitcast.4) | data formatting | bytes 2097152 | tf_op jit(solution)/shard_map/transpose | solution.py:478
  63.1 1.3 copy.6.own_ref
  64.4 123.9 %shard_map.38 = f32[64,8192]{1,0:T(8,128)} custom-call(bf16[8192,4096]{1,0:T(8,128)(2,1)} %a_ref.1, bf16[8,128,512]{2,1,0:T(8,128)(2,1)} %copy.6.own_ref), custom_call_target="tpu_custom_call" | custom-call | tf_op jit(solution)/shard_map/pallas_call | solution.py:445
  188.3 3.1 %copy.8 = f32[8192,64]{0,1:T(8,128)} copy(f32[8192,64]{0,1:T(8,128)} %bitcast.3) | data formatting | bytes 4194304
